TPU v7x, 512 devices: a whole 4x8x8 slice. The times are simulated.
512 devices in a mesh: tm: 64 (over z, y), chan: 8 (over x, core).
Axes of the slice: x: 4, y: 8, z: 8, core: 2. Of those that a mesh axis runs over, the one named last changes fastest.
Arguments:
- values: bfloat16 [16384, 4096], P('tm', 'chan'), may hold values from -6 to 6
- gates: bfloat16 [16384, 4096], P('tm', 'chan'), may hold values from -6 to 6
- cotangent: bfloat16 [16384, 4096], P('tm', 'chan'), may hold values from -6 to 6
- kernel_taps: bfloat16 [256, 4096], P(None, 'chan'), may hold values from -0.375 to 0.375
- value_weight: bfloat16 [4096, 4096], P('tm', 'chan'), may hold values from -0.09375 to 0.09375
- gate_weight: bfloat16 [4096, 4096], P('tm', 'chan'), may hold values from -0.09375 to 0.09375
Outputs:
- grad_input: bfloat16 [16384, 4096], P('tm', 'chan')
- kernel_grad: float32 [256, 4096], P('tm', 'chan')
All inputs are finite; a program needn't handle non-finite values.
Results may differ from a plain program's by a relative error of at most 0.017.
Values may be sent and summed in bfloat16 or wider, within the bound.
A program may use at most 64 MiB of HBM per device.

v0:
```python
import math
import jax
import jax.numpy as jnp
import numpy as np
from jax import lax
from jax.sharding import PartitionSpec as P


def from_behind(value, axis, steps):
    count = lax.axis_size(axis)
    initial, last = (max(0, -steps), min(count, count - steps))
    return lax.ppermute(value, axis, [(source, source + steps) for source in range(initial, last)])


def contract_rows(left, weight_rows):
    return lax.dot_general(
        left, weight_rows, (((1,), (1,)), ((), ())), preferred_element_type=jnp.float32
    )


def forward_tables(length):
    freq_count = length // 2 + 1
    phase = np.arange(freq_count)[:, None] * np.arange(length)[None, :] % length
    angle = phase * (2.0 * np.pi / length)
    return (
        jnp.asarray(np.cos(angle), dtype=jnp.float32),
        jnp.asarray(np.sin(angle), dtype=jnp.float32),
    )


def inverse_tables(first, count, length):
    freq_count = length // 2 + 1
    freqs = np.arange(freq_count)
    phase = (first + np.arange(count))[:, None] * freqs[None, :] % length
    angle = phase * (2.0 * np.pi / length)
    weight = np.where((freqs == 0) | (freqs == length // 2), 1.0, 2.0) / length
    return (
        jnp.asarray(np.cos(angle) * weight[None, :], dtype=jnp.float32),
        jnp.asarray(np.sin(angle) * weight[None, :], dtype=jnp.float32),
    )


def precise_dot(left, right):
    return jnp.dot(left, right, precision=lax.Precision.HIGHEST, preferred_element_type=jnp.float32)


def back_to_time(first, count, length, real_part, imag_part):
    cos_inv, sin_inv = inverse_tables(first, count, length)
    return precise_dot(cos_inv, real_part) - precise_dot(sin_inv, imag_part)


def body(values, gates, cotangent, kernel_taps, value_weight, gate_weight):
    row_count, chan_count = values.shape
    span_len = kernel_taps.shape[0]
    window_len = row_count + span_len
    grad_conv = (cotangent.astype(jnp.float32) * gates.astype(jnp.float32)).astype(jnp.bfloat16)
    value_rim = from_behind(values[row_count - span_len + 1 :], "tm", 1)
    grad_rim = from_behind(grad_conv[: span_len - 1], "tm", -1)
    zero_row = jnp.zeros((1, chan_count), jnp.bfloat16)
    value_window = jnp.concatenate([zero_row, value_rim, values], 0)
    grad_window = jnp.concatenate([grad_conv, grad_rim, zero_row], 0)
    grad_padded = jnp.concatenate([jnp.zeros((span_len, chan_count), jnp.bfloat16), grad_conv], 0)
    taps_padded = jnp.concatenate(
        [kernel_taps, jnp.zeros((row_count, chan_count), jnp.bfloat16)], 0
    )
    joined_time = jnp.concatenate([value_window, grad_window, grad_padded, taps_padded], 1).astype(
        jnp.float32
    )
    cos_fwd, sin_fwd = forward_tables(window_len)
    real_all = precise_dot(cos_fwd, joined_time)
    imag_all = -precise_dot(sin_fwd, joined_time)
    value_re = real_all[:, :chan_count]
    value_im = imag_all[:, :chan_count]
    grad_re = real_all[:, chan_count : 2 * chan_count]
    grad_im = imag_all[:, chan_count : 2 * chan_count]
    pad_re = real_all[:, 2 * chan_count : 3 * chan_count]
    pad_im = imag_all[:, 2 * chan_count : 3 * chan_count]
    taps_re = real_all[:, 3 * chan_count :]
    taps_im = imag_all[:, 3 * chan_count :]
    conv_out = back_to_time(
        span_len,
        row_count,
        window_len,
        value_re * taps_re - value_im * taps_im,
        value_re * taps_im + value_im * taps_re,
    )
    grad_value = back_to_time(
        0,
        row_count,
        window_len,
        grad_re * taps_re + grad_im * taps_im,
        grad_im * taps_re - grad_re * taps_im,
    ).astype(jnp.bfloat16)
    norm_scale = 1.0 / math.sqrt(row_count * lax.axis_size("tm"))
    kernel_part = (
        back_to_time(
            0,
            span_len,
            window_len,
            pad_re * value_re + pad_im * value_im,
            pad_im * value_re - pad_re * value_im,
        )
        * norm_scale
    )
    grad_gate = (cotangent.astype(jnp.float32) * conv_out).astype(jnp.bfloat16)
    kernel_grad = lax.psum_scatter(kernel_part, "tm", scatter_dimension=0, tiled=True)
    terms = contract_rows(grad_value, lax.all_gather(value_weight, "tm", axis=0, tiled=True))
    terms = terms + contract_rows(grad_gate, lax.all_gather(gate_weight, "tm", axis=0, tiled=True))
    grad_input = lax.psum_scatter(
        terms.astype(jnp.bfloat16), "chan", scatter_dimension=1, tiled=True
    )
    return (grad_input, kernel_grad)


def solution(mesh):
    placed = (
        P("tm", "chan"),
        P("tm", "chan"),
        P("tm", "chan"),
        P(None, "chan"),
        P("tm", "chan"),
        P("tm", "chan"),
    )
    return jax.shard_map(
        body,
        mesh=mesh,
        in_specs=placed,
        out_specs=(P("tm", "chan"), P("tm", "chan")),
        check_vma=False,
    )
```

profile of v0, /device:TPU:8, one launch (start us, length us, event | category | flops | bytes accessed | tf_op | source)
XLA Modules:
  0.0 391.1 jit_solution(17819899406508750567)
XLA Ops:
  7.2 0.0 all-gather.3.cloned.1.call-start
  7.2 0.7 all-gather.3.cloned.1.call-update
  7.9 0.0 all-gather.5.cloned.1.call-start
  7.9 0.7 all-gather.5.cloned.1.call-update
  8.6 0.0 all-reduce.5.cloned.1.call-start
  8.7 1.0 slice.30
  9.7 0.0 copy-start.5
  9.7 3.6 collective-permute-start
  13.3 1.1 fusion.34
  14.4 5.6 %collective-permute-start.1 = (bf16[255,512]{1,0:T(8,128)(2,1)S(1)}, bf16[255,512]{1,0:T(8,128)(2,1)S(1)}, u32[]{:S(2)}, u32[]{:S(2)}) collective-permute-start(bf16[255,512]{1,0:T(8,128)(2,1)S(1)} %bitcast.28), channel_id=1, source_target_pairs={{8,0},{16,8},{24,16},{32,24},{40,32},{48,40},{56,48},{64,56},{72,6... | collective-permute-start | bytes 783368 | tf_op jit(solution)/shard_map/ppermute | solution.py:12
  20.0 1.3 collective-permute-done
  21.3 2.8 collective-permute-done.1
  24.1 4.9 %fusion.6 = bf16[512,2048]{1,0:T(8,128)(2,1)S(1)} fusion(bf16[256,512]{1,0:T(8,128)(2,1)} %param.17, bf16[256,512]{1,0:T(8,128)(2,1)S(1)} %fusion.34, bf16[1,512]{1,0:T(2,128)(2,1)S(1)} %broadcast_in_dim.3, bf16[255,512]{1,0:T(8,128)(2,1)S(1)} %collective-permute-done.1, bf16[256,512]{1,0:T(8,128)(2,1)} %param.14, bf16[255,512]{1,0:T(8,128)(2,1)S(1)} %collective-permute-done), kind=kLoop, calls=%fused_computation.11 | loop fusion | flops 23068672 | bytes 3406848 | tf_op jit(solution)/shard_map/concatenate | solution.py:66
  29.0 0.0 copy-done.5
  29.0 0.0 copy-start.3
  29.0 1.9 fusion.4
  30.9 0.0 copy-done.3
  30.9 0.0 copy-start
  30.9 0.0 copy-start.2
  30.9 1.9 fusion.59
  32.8 0.0 copy-done.2
  32.8 0.0 copy-start.6
  32.8 1.5 fusion.16
  34.3 0.0 copy-start.1
  34.3 1.5 fusion.30
  35.8 0.0 copy-done.6
  35.8 1.1 fusion.23
  37.0 0.0 copy-done.1
  37.0 0.0 copy-start.4
  37.0 1.5 fusion.12
  38.5 0.0 copy-done
  38.5 2.3 fusion.8
  40.8 0.0 all-reduce.5.cloned.1.call-update
  40.8 0.3 reduce-scatter.3.cloned.1.call-start
  41.1 0.0 copy-done.4
  41.1 2.4 fusion.11
  43.5 59.0 %all-gather.3.cloned.1.call-done = bf16[4096,512]{1,0:T(8,128)(2,1)} async-done(((bf16[64,512]{1,0:T(8,128)(2,1)}), bf16[4096,512]{1,0:T(8,128)(2,1)}) %all-gather.3.cloned.1.call-update) | async-done | bytes 4194320 | tf_op jit(solution)/shard_map/all_gather | solution.py:107
  102.5 5.5 %fusion.60 = f32[256,4096]{1,0:T(8,128)} fusion(bf16[512,256]{1,0:T(8,128)(2,1)S(1)} %fusion.12, bf16[4096,512]{1,0:T(8,128)(2,1)} %all-gather.3.cloned.1.call-done), kind=kOutput, calls=%fused_computation.70 | convolution fusion | flops 1073741824 | bytes 8650752 | tf_op jit(solution)/shard_map/dot_general | solution.py:16
  108.0 81.5 %all-gather.5.cloned.1.call-done = bf16[4096,512]{1,0:T(8,128)(2,1)} async-done(((bf16[64,512]{1,0:T(8,128)(2,1)}), bf16[4096,512]{1,0:T(8,128)(2,1)}) %all-gather.5.cloned.1.call-update) | async-done | bytes 4194320 | tf_op jit(solution)/shard_map/all_gather | solution.py:108
  189.5 6.1 %fusion = bf16[256,4096]{1,0:T(8,128)(2,1)} fusion(f32[256,4096]{1,0:T(8,128)} %fusion.60, bf16[256,512]{1,0:T(8,128)(2,1)S(1)} %fusion.11, bf16[4096,512]{1,0:T(8,128)(2,1)} %all-gather.5.cloned.1.call-done), kind=kOutput, calls=%fused_computation.3 | convolution fusion | flops 1075838976 | bytes 10747904 | tf_op jit(solution)/shard_map/dot_general | solution.py:16
  195.5 0.0 reduce-scatter.3.cloned.1.call-update
  195.6 1.3 dynamic-slice
  197.5 147.6 %all-reduce.5.cloned.1.call-done = f32[256,512]{0,1:T(8,128)} async-done(((f32[256,512]{0,1:T(8,128)}), f32[256,512]{0,1:T(8,128)}) %all-reduce.5.cloned.1.call-update) | async-done | bytes 524304
  345.1 1.1 constant_dynamic-slice_fusion
  346.2 0.7 copy.17
  346.9 37.6 %reduce-scatter.3.cloned.1.call-done = bf16[256,512]{1,0:T(8,128)(2,1)} async-done(((bf16[256,4096]{1,0:T(8,128)(2,1)}), bf16[256,512]{1,0:T(8,128)(2,1)}) %reduce-scatter.3.cloned.1.call-update) | async-done | bytes 262160 | tf_op jit(solution)/shard_map/reduce_scatter | solution.py:109
  (1 shorter events, 0.0 us)
Async XLA Ops:
  7.2 95.4 %all-gather.3.cloned.1.call-start = ((), (), s32[]{:S(2)}) async-start(), calls=%async_computation.1 | async-start | bytes 4259840 | tf_op jit(solution)/shard_map/all_gather | solution.py:107
  7.9 181.6 %all-gather.5.cloned.1.call-start = ((), (), s32[]{:S(2)}) async-start(), calls=%async_computation.2 | async-start | bytes 4259840 | tf_op jit(solution)/shard_map/all_gather | solution.py:108
  8.6 336.5 %all-reduce.5.cloned.1.call-start = ((), (), s32[]{:S(2)}) async-start(), calls=%async_computation.4 | async-start | bytes 1048576
  9.7 19.3 %copy-start.5 = (f32[257,512]{1,0:T(8,128)S(1)}, f32[257,512]{1,0:T(8,128)}, u32[]{:S(2)}) copy-start(f32[257,512]{1,0:T(8,128)} %constant.18.clone) | copy-start | bytes 1579012
  9.7 11.6 %collective-permute-start = (bf16[255,512]{1,0:T(8,128)(2,1)S(1)}, bf16[255,512]{1,0:T(8,128)(2,1)S(1)}, u32[]{:S(2)}, u32[]{:S(2)}) collective-permute-start(bf16[255,512]{1,0:T(8,128)(2,1)S(1)} %slice.30), channel_id=1, source_target_pairs={{0,8},{8,16},{16,24},{24,32},{32,40},{40,48},{48,56},{56,64},{64,7... | collective-permute-start | bytes 783368 | tf_op jit(solution)/shard_map/ppermute | solution.py:12
  14.4 9.7 %collective-permute-start.1 = (bf16[255,512]{1,0:T(8,128)(2,1)S(1)}, bf16[255,512]{1,0:T(8,128)(2,1)S(1)}, u32[]{:S(2)}, u32[]{:S(2)}) collective-permute-start(bf16[255,512]{1,0:T(8,128)(2,1)S(1)} %bitcast.28), channel_id=1, source_target_pairs={{8,0},{16,8},{24,16},{32,24},{40,32},{48,40},{56,48},{64,56},{72,6... | collective-permute-start | bytes 783368 | tf_op jit(solution)/shard_map/ppermute | solution.py:12
  29.0 1.9 copy-start.3
  30.9 7.6 %copy-start = (f32[257,2048]{1,0:T(8,128)}, f32[257,2048]{1,0:T(8,128)S(1)}, u32[]{:S(2)}) copy-start(f32[257,2048]{1,0:T(8,128)S(1)} %fusion.4) | copy-start | bytes 6316036
  30.9 1.9 copy-start.2
  32.8 3.0 copy-start.6
  34.3 2.6 copy-start.1
  37.0 4.1 %copy-start.4 = (bf16[256,512]{1,0:T(8,128)(2,1)S(1)}, bf16[256,512]{1,0:T(8,128)(2,1)}, u32[]{:S(2)}) copy-start(bf16[256,512]{1,0:T(8,128)(2,1)} %param.16) | copy-start | bytes 786436
  40.8 343.7 %reduce-scatter.3.cloned.1.call-start = ((), (), s32[]{:S(2)}) async-start(), calls=%async_computation.3 | async-start | bytes 2359296 | tf_op jit(solution)/shard_map/reduce_scatter | solution.py:109
Sparse Core Ops, SparseCore 0:
  11.1 91.4 all-gather.2
  105.6 83.8 all-gather.4
  192.7 152.4 all-reduce.4
  348.6 35.8 reduce-scatter.2
where the time goes:
time: 391 us
  waiting for transfers between devices  331 us (85%)
  matrix products  25.6 us (7%)
  between operations  14.6 us (4%)
  starting transfers between devices  9.54 us (2%)
  other arithmetic  5.97 us (2%)
  local copies, waits for them, and re-layouts  4.12 us (1%)
    unnamed x5, waiting for transfers between devices  149 us
    all_gather x1, waiting for transfers between devices, body(): lax.all_gather(gate_weight, 'tm', axis=0, tiled=True)  81.5 us
    all_gather x1, waiting for transfers between devices, body(): lax.all_gather(value_weight, 'tm', axis=0, tiled=True)  59 us
    reduce_scatter x1, waiting for transfers between devices, body(): lax.psum_scatter(terms.astype(jnp.bfloat16), 'chan', scatter_dimension=1,...  37.6 us
    dot_general x8, matrix products, precise_dot(): jnp.dot(left, right, precision=lax.Precision.HIGHEST, preferred_element_t...  14.1 us
    dot_general x2, matrix products, contract_rows(): lax.dot_general(left, weight_rows, (((1,), (1,)), ((), ())), preferred_el...  11.6 us
    ppermute x2, starting transfers between devices, from_behind(): lax.ppermute(value, axis, [(source, source + steps) for source in range(i...  9.17 us
  transfers between devices with their start and end apart: 6, of which 6 were waited for; matrix products, arithmetic and copies ran while one was open for 9% of the time, Pallas kernels for 0%

commit v1 on v0

--- a/solution.py
+++ b/solution.py
@@ -104,7 +104,12 @@
     )
     grad_gate = (cotangent.astype(jnp.float32) * conv_out).astype(jnp.bfloat16)
     kernel_grad = lax.psum_scatter(kernel_part, "tm", scatter_dimension=0, tiled=True)
-    terms = contract_rows(grad_value, lax.all_gather(value_weight, "tm", axis=0, tiled=True))
+    terms = contract_rows(
+        grad_value,
+        jnp.concatenate(
+            lax.all_to_all(jnp.stack([value_weight] * lax.axis_size("tm")), "tm", 0, 0), axis=0
+        ),
+    )
     terms = terms + contract_rows(grad_gate, lax.all_gather(gate_weight, "tm", axis=0, tiled=True))
     grad_input = lax.psum_scatter(
         terms.astype(jnp.bfloat16), "chan", scatter_dimension=1, tiled=True

time: 391 us -> 400 us (1.023)
  starting transfers between devices: 9.54 us -> 23.2 us
  waiting for transfers between devices: 331 us -> 321 us
    ppermute x2, waiting for transfers between devices: 4.1 us -> 121 us  [from_behind(): lax.ppermute(value, axis, [(source, source + steps) for source in range(i...]
    all_gather x1, waiting for transfers between devices: 81.5 us -> 13.6 us  [body(): lax.all_gather(gate_weight, 'tm', axis=0, tiled=True)]
    all_gather x1 -> x0, waiting for transfers between devices: 59 us -> none  [body(): lax.all_gather(value_weight, 'tm', axis=0, tiled=True)]
    all_to_all x0 -> x1, starting transfers between devices: none -> 16.9 us  [body(): lax.all_to_all(jnp.stack([value_weight] * lax.axis_size('tm')), 'tm', 0, 0)]
    unnamed x5 -> x4, waiting for transfers between devices: 149 us -> 148 us
  transfers between devices with their start and end apart: 6 -> 6, of which waited for: 6 -> 4; matrix products, arithmetic and copies ran while one was open for 9% -> 10% of each run, Pallas kernels for 0% -> 0%
where the time goes in v1:
time: 400 us; the launch traced here: 399 us
  waiting for transfers between devices  321 us (80%)
  matrix products  27.1 us (7%)
  starting transfers between devices  23.2 us (6%)
  between operations  14.7 us (4%)
  other arithmetic  7.11 us (2%)
  local copies, waits for them, and re-layouts  6.49 us (2%)
    unnamed x4, waiting for transfers between devices  148 us
    ppermute x2, waiting for transfers between devices, from_behind(): lax.ppermute(value, axis, [(source, source + steps) for source in range(i...  121 us
    reduce_scatter x1, waiting for transfers between devices, body(): lax.psum_scatter(terms.astype(jnp.bfloat16), 'chan', scatter_dimension=1,...  37.8 us
    all_to_all x1, starting transfers between devices, body(): lax.all_to_all(jnp.stack([value_weight] * lax.axis_size('tm')), 'tm', 0, 0)  16.9 us
    dot_general x8, matrix products, precise_dot(): jnp.dot(left, right, precision=lax.Precision.HIGHEST, preferred_element_t...  15.5 us
    all_gather x1, waiting for transfers between devices, body(): lax.all_gather(gate_weight, 'tm', axis=0, tiled=True)  13.6 us
    dot_general x2, matrix products, contract_rows(): lax.dot_general(left, weight_rows, (((1,), (1,)), ((), ())), preferred_el...  11.6 us
  transfers between devices with their start and end apart: 6, of which 4 were waited for; matrix products, arithmetic and copies ran while one was open for 10% of the time, Pallas kernels for 0%

profile of v1, /device:TPU:8, one launch (start us, length us, event | category | flops | bytes accessed | tf_op | source)
XLA Modules:
  0.0 399.4 jit_solution(12722056661733368587)
XLA Ops:
  7.2 0.0 all-gather.2.cloned.1.call-start
  7.2 0.7 all-gather.2.cloned.1.call-update
  7.9 3.3 stack.2
  11.2 16.9 %all-to-all-start = ((bf16[64,64,512]{2,1,0:T(8,128)(2,1)}), bf16[64,64,512]{2,1,0:T(8,128)(2,1)}, u32[]{:S(2)}, u32[]{:S(2)}) async-start(bf16[64,64,512]{2,1,0:T(8,128)(2,1)} %stack.2), calls=%async_computation | async-start | bytes 8388608 | tf_op jit(solution)/shard_map/all_to_all | solution.py:110
  28.1 0.0 all-reduce.5.cloned.1.call-start
  28.2 0.0 copy-done.6
  28.2 0.1 slice.30
  28.3 0.0 copy-start.7
  28.3 3.5 collective-permute-start
  31.8 0.0 copy-done.5
  31.8 0.0 copy-done.9
  31.8 0.1 fusion.34
  31.9 2.5 collective-permute-start.1
  34.4 121.1 %collective-permute-done = bf16[255,512]{1,0:T(8,128)(2,1)S(1)} collective-permute-done((bf16[255,512]{1,0:T(8,128)(2,1)S(1)}, bf16[255,512]{1,0:T(8,128)(2,1)S(1)}, u32[]{:S(2)}, u32[]{:S(2)}) %collective-permute-start) | collective-permute-done | bytes 261152 | tf_op jit(solution)/shard_map/ppermute | solution.py:12
  155.5 0.0 collective-permute-done.1
  155.5 0.0 copy-done.10
  155.5 7.0 %fusion.6 = bf16[512,2048]{1,0:T(8,128)(2,1)S(1)} fusion(bf16[256,512]{1,0:T(8,128)(2,1)S(1)} %copy-done.10, bf16[256,512]{1,0:T(8,128)(2,1)S(1)} %fusion.34, bf16[1,512]{1,0:T(2,128)(2,1)S(1)} %broadcast_in_dim.3, bf16[255,512]{1,0:T(8,128)(2,1)S(1)} %collective-permute-done.1, bf16[256,512]{1,0:T(8,128)(2,1)S(1)} %copy-done.6, ...), kind=kLoop, calls=%fused_computation.11 | loop fusion | flops 23068672 | bytes 3406848 | tf_op jit(solution)/shard_map/concatenate | solution.py:66
  162.6 0.0 copy-done.7
  162.6 0.0 copy-start.4
  162.6 1.9 fusion.4
  164.5 0.0 copy-done.4
  164.5 0.0 copy-start
  164.5 0.0 copy-start.3
  164.5 1.9 fusion.59
  166.4 0.0 copy-done.3
  166.4 0.0 copy-start.2
  166.4 1.5 fusion.16
  167.9 0.0 copy-done
  167.9 0.0 copy-done.2
  167.9 2.3 fusion.8
  170.2 0.0 all-reduce.5.cloned.1.call-update
  170.3 0.2 reduce-scatter.3.cloned.1.call-start
  170.5 0.0 copy-start.1
  170.5 2.9 fusion.30
  173.4 0.0 copy-start.8
  173.4 2.5 fusion.23
  175.9 1.5 fusion.12
  177.4 1.1 fusion.11
  178.5 0.0 all-to-all-done
  178.5 5.5 %fusion.60 = f32[256,4096]{1,0:T(8,128)} fusion(bf16[512,256]{1,0:T(8,128)(2,1)S(1)} %fusion.12, bf16[4096,512]{1,0:T(8,128)(2,1)} %bitcast.1), kind=kOutput, calls=%fused_computation.70 | convolution fusion | flops 1073741824 | bytes 8650752 | tf_op jit(solution)/shard_map/dot_general | solution.py:16
  184.0 13.6 %all-gather.2.cloned.1.call-done = bf16[4096,512]{1,0:T(8,128)(2,1)} async-done(((bf16[64,512]{1,0:T(8,128)(2,1)}), bf16[4096,512]{1,0:T(8,128)(2,1)}) %all-gather.2.cloned.1.call-update) | async-done | bytes 4194320 | tf_op jit(solution)/shard_map/all_gather | solution.py:113
  197.6 6.1 %fusion = bf16[256,4096]{1,0:T(8,128)(2,1)} fusion(f32[256,4096]{1,0:T(8,128)} %fusion.60, bf16[256,512]{1,0:T(8,128)(2,1)S(1)} %fusion.11, bf16[4096,512]{1,0:T(8,128)(2,1)} %all-gather.2.cloned.1.call-done), kind=kOutput, calls=%fused_computation.3 | convolution fusion | flops 1075838976 | bytes 10747904 | tf_op jit(solution)/shard_map/dot_general | solution.py:16
  203.7 0.0 reduce-scatter.3.cloned.1.call-update
  203.7 1.3 dynamic-slice
  205.7 147.6 %all-reduce.5.cloned.1.call-done = f32[256,512]{0,1:T(8,128)} async-done(((f32[256,512]{0,1:T(8,128)}), f32[256,512]{0,1:T(8,128)}) %all-reduce.5.cloned.1.call-update) | async-done | bytes 524304
  353.3 1.1 constant_dynamic-slice_fusion
  354.4 0.7 copy.17
  355.1 37.8 %reduce-scatter.3.cloned.1.call-done = bf16[256,512]{1,0:T(8,128)(2,1)} async-done(((bf16[256,4096]{1,0:T(8,128)(2,1)}), bf16[256,512]{1,0:T(8,128)(2,1)}) %reduce-scatter.3.cloned.1.call-update) | async-done | bytes 262160 | tf_op jit(solution)/shard_map/reduce_scatter | solution.py:114
  (7 shorter events, 0.0 us)
Async XLA Ops:
  7.2 190.4 %all-gather.2.cloned.1.call-start = ((), (), s32[]{:S(2)}) async-start(), calls=%async_computation.2 | async-start | bytes 4259840 | tf_op jit(solution)/shard_map/all_gather | solution.py:113
  11.2 17.0 %copy-start.6 = (bf16[256,512]{1,0:T(8,128)(2,1)S(1)}, bf16[256,512]{1,0:T(8,128)(2,1)}, u32[]{:S(2)}) copy-start(bf16[256,512]{1,0:T(8,128)(2,1)} %param.14) | copy-start | bytes 786436
  11.2 20.6 %copy-start.5 = (bf16[256,512]{1,0:T(8,128)(2,1)S(1)}, bf16[256,512]{1,0:T(8,128)(2,1)}, u32[]{:S(2)}) copy-start(bf16[256,512]{1,0:T(8,128)(2,1)} %param.16) | copy-start | bytes 786436
  11.2 20.6 %copy-start.9 = (bf16[256,512]{1,0:T(8,128)(2,1)S(1)}, bf16[256,512]{1,0:T(8,128)(2,1)}, u32[]{:S(2)}) copy-start(bf16[256,512]{1,0:T(8,128)(2,1)} %param.15) | copy-start | bytes 786436
  11.2 144.3 %copy-start.10 = (bf16[256,512]{1,0:T(8,128)(2,1)S(1)}, bf16[256,512]{1,0:T(8,128)(2,1)}, u32[]{:S(2)}) copy-start(bf16[256,512]{1,0:T(8,128)(2,1)} %param.17) | copy-start | bytes 786436
  11.2 167.3 %all-to-all-start = ((bf16[64,64,512]{2,1,0:T(8,128)(2,1)}), bf16[64,64,512]{2,1,0:T(8,128)(2,1)}, u32[]{:S(2)}, u32[]{:S(2)}) async-start(bf16[64,64,512]{2,1,0:T(8,128)(2,1)} %stack.2), calls=%async_computation | async-start | bytes 8388608 | tf_op jit(solution)/shard_map/all_to_all | solution.py:110
  28.1 325.2 %all-reduce.5.cloned.1.call-start = ((), (), s32[]{:S(2)}) async-start(), calls=%async_computation.4 | async-start | bytes 1048576
  28.3 134.3 %copy-start.7 = (f32[257,512]{1,0:T(8,128)S(1)}, f32[257,512]{1,0:T(8,128)}, u32[]{:S(2)}) copy-start(f32[257,512]{1,0:T(8,128)} %constant.18.clone) | copy-start | bytes 1579012
  28.3 127.2 %collective-permute-start = (bf16[255,512]{1,0:T(8,128)(2,1)S(1)}, bf16[255,512]{1,0:T(8,128)(2,1)S(1)}, u32[]{:S(2)}, u32[]{:S(2)}) collective-permute-start(bf16[255,512]{1,0:T(8,128)(2,1)S(1)} %slice.30), channel_id=1, source_target_pairs={{0,8},{8,16},{16,24},{24,32},{32,40},{40,48},{48,56},{56,64},{64,7... | collective-permute-start | bytes 783368 | tf_op jit(solution)/shard_map/ppermute | solution.py:12
  31.9 123.6 %collective-permute-start.1 = (bf16[255,512]{1,0:T(8,128)(2,1)S(1)}, bf16[255,512]{1,0:T(8,128)(2,1)S(1)}, u32[]{:S(2)}, u32[]{:S(2)}) collective-permute-start(bf16[255,512]{1,0:T(8,128)(2,1)S(1)} %bitcast.29), channel_id=1, source_target_pairs={{8,0},{16,8},{24,16},{32,24},{40,32},{48,40},{56,48},{64,56},{72,6... | collective-permute-start | bytes 783368 | tf_op jit(solution)/shard_map/ppermute | solution.py:12
  162.6 1.9 copy-start.4
  164.5 3.4 copy-start
  164.5 1.9 copy-start.3
  166.4 1.5 copy-start.2
  170.3 222.6 %reduce-scatter.3.cloned.1.call-start = ((), (), s32[]{:S(2)}) async-start(), calls=%async_computation.3 | async-start | bytes 2359296 | tf_op jit(solution)/shard_map/reduce_scatter | solution.py:114
  170.5 5.4 %copy-start.1 = (f32[257,2048]{1,0:T(8,128)S(1)}, f32[257,2048]{1,0:T(8,128)}, u32[]{:S(2)}) copy-start(f32[257,2048]{1,0:T(8,128)} %copy-done) | copy-start | bytes 6316036
  173.4 4.0 copy-start.8
Sparse Core Ops, SparseCore 0:
  11.1 186.4 all-gather.1
  200.8 152.4 all-reduce.4
  357.0 35.8 reduce-scatter.2
